TPU v7x, 32 devices: a whole 2x2x4 slice. The times are simulated.
32 devices in a mesh: row: 4 (over z), col: 2 (over x), pole: 4 (over y, core).
Axes of the slice: x: 2, y: 2, z: 4, core: 2. Of those that a mesh axis runs over, the one named last changes fastest.
Arguments:
- window: bfloat16 [4, 8192, 8192], P('pole', 'col', 'row'), may hold values from -6 to 6
- panels: bfloat16 [4, 2, 8192, 256], P('pole', 'col', 'row'), may hold values from -0.0625 to 0.0625
- row_map: int32 [3, 8192], P(None, 'row'), may hold values from 0 to 8191, as said below
- panel_root: int32 [4, 3], P('pole'), may hold values from 0 to 1
- upper_blocks: bfloat16 [4, 3, 256, 256], P('pole', None, 'row'), may hold values from -0.375 to 0.375
- diag_inverse: float32 [4, 3, 256, 256], P('pole', None, 'row'), may hold values from -6 to 6
- weights: float32 [4], replicated, may hold values from 0.25 to 1
- pole_order: int32 [4], P('pole'), may hold values from 0 to 3, each once
Outputs:
- inv_columns: float32 [3, 2, 4096, 256], P(None, 'col', ('row', 'pole'))
- inv_diag: float32 [3, 256, 256], P(None, ('row', 'pole'))
Inputs may be any that keep to these rules, and one draw needn't show every extreme that they name: row_map[k] permutes the positions inside each aligned group of 1024 consecutive positions. `pole_order`: each of the 4 poles appears once.
All inputs are finite; a program needn't handle non-finite values.
Results may differ from a plain program's by a relative error of at most 0.0003.
Values may be sent and summed in bfloat16 or wider, within the bound.
A program may use at most 128 MiB of HBM per device.

v0:
```python
import jax
import jax.numpy as jnp
from jax import lax
from jax.sharding import PartitionSpec as P

NS = 3


def precise(left, right):
    return jnp.dot(left, right, precision=lax.Precision.HIGHEST, preferred_element_type=jnp.float32)


def pair_index(current, earlier):
    return current * (current - 1) // 2 + earlier


def inverse_block(diagonals, crossed, first, second):
    if first == second:
        return diagonals[first]
    if first < second:
        return crossed[first, second]
    return crossed[second, first].T


def window_term(window_block, aligned):
    return jnp.dot(window_block, aligned, preferred_element_type=jnp.float32)


def shards(window, panels, row_map, panel_root, upper_blocks, diag_inverse, weights, pole_order):
    window_block = window[0]
    panel_slab = panels[0, 0]
    pole_roots = panel_root[0]
    band_rows = panel_slab.shape[0]
    group_rows = window_block.shape[0] // lax.axis_size("row")
    row_index = lax.axis_index("row")
    col_index = lax.axis_index("col")
    gathered_upper, gathered_inverse = (
        lax.all_gather(upper_blocks.astype(jnp.float32), "row", axis=2, tiled=True).astype(
            upper_blocks.dtype
        ),
        lax.all_gather(diag_inverse, "row", axis=2, tiled=True),
    )
    factors = gathered_upper[0].astype(jnp.float32)
    inverses = gathered_inverse[0]
    share_rows = inverses.shape[1] // lax.axis_size("row")
    slot_panels = lax.all_gather(panels, "col", axis=1, tiled=True)[0]
    pole_weight = jnp.sum(jnp.where(jnp.arange(weights.shape[0]) == pole_order[0], weights, 0.0))
    columns = []
    diagonals = []
    crossed = {}
    for current in range(NS):
        received = lax.dynamic_index_in_dim(slot_panels, pole_roots[current], 0, keepdims=False)
        aligned = jnp.take(received, row_map[current] - row_index * band_rows, axis=0)
        own_rows = lax.dynamic_slice_in_dim(aligned, col_index * group_rows, group_rows, 0).astype(
            jnp.float32
        )
        partials = [precise(columns[earlier].T, own_rows) for earlier in range(current)]
        window_sum = lax.psum_scatter(
            window_term(window_block, aligned), "row", scatter_dimension=0, tiled=True
        )
        y_window = window_sum
        for earlier in range(current):
            y_window = y_window + precise(columns[earlier], factors[pair_index(current, earlier)])
        congruence = precise(own_rows.T, y_window)
        stacked = lax.psum(jnp.stack(partials + [congruence]), ("row", "col"))
        summed_cross = stacked[:current]
        summed_own = stacked[current]
        y_blocks = []
        for earlier in range(current):
            block_sum = summed_cross[earlier]
            for other_node in range(current):
                block_sum = block_sum + precise(
                    inverse_block(diagonals, crossed, earlier, other_node),
                    factors[pair_index(current, other_node)],
                )
            y_blocks.append(block_sum)
        diagonal = inverses[current] + summed_own
        for earlier in range(current):
            diagonal = diagonal + precise(
                factors[pair_index(current, earlier)].T, y_blocks[earlier]
            )
            crossed[earlier, current] = -y_blocks[earlier]
        columns.append(-y_window)
        diagonals.append(diagonal)
    column_terms = jnp.stack(columns) * pole_weight
    diagonal_terms = (
        jnp.stack(
            [
                lax.dynamic_slice_in_dim(diagonal, row_index * share_rows, share_rows, 0)
                for diagonal in diagonals
            ]
        )
        * pole_weight
    )
    summed_columns, summed_diagonals = (
        lax.psum_scatter(column_terms, "pole", scatter_dimension=1, tiled=True),
        lax.psum_scatter(diagonal_terms, "pole", scatter_dimension=1, tiled=True),
    )
    return (summed_columns[:, None], summed_diagonals)


def solution(mesh):
    return jax.shard_map(
        shards,
        mesh=mesh,
        in_specs=(
            P("pole", "col", "row"),
            P("pole", "col", "row", None),
            P(None, "row"),
            P("pole", None),
            P("pole", None, "row", None),
            P("pole", None, "row", None),
            P(),
            P("pole"),
        ),
        out_specs=(P(None, "col", ("row", "pole"), None), P(None, ("row", "pole"), None)),
        check_vma=False,
    )
```

profile of v0, /device:TPU:0, one launch (start us, length us, event | category | flops | bytes accessed | tf_op | source)
XLA Modules:
  0.0 490.8 jit_solution(11846383781759528025)
XLA Ops:
  7.9 1.4 fusion.45
  16.0 29.3 %all-gather.2.cloned.1.call-done = bf16[1,2,2048,256]{3,2,0,1:T(8,128)(2,1)} async-done(((bf16[1,1,2048,256]{3,2,0,1:T(8,128)(2,1)}), bf16[1,2,2048,256]{3,2,0,1:T(8,128)(2,1)}) %all-gather.2.cloned.1.call-update) | async-done | bytes 2097168 | tf_op jit(solution)/shard_map/all_gather | solution.py:46
  45.4 2.2 dynamic-slice_bitcast_fusion.1
  47.6 9.0 %gather_fusion = bf16[2048,256]{1,0:T(8,128)(2,1)} fusion(bf16[2048,256]{1,0:T(8,128)(2,1)S(1)} %get-tuple-element.12, s32[2048]{0:T(1024)S(1)} %fusion.35), kind=kCustom, calls=%fused_computation.clone | custom fusion | bytes 2105344 | tf_op jit(solution)/shard_map/jit(_take)/gather | solution.py:53
  56.6 1.5 broadcast_select_fusion.2
  58.1 10.5 %fusion.6 = f32[4096,256]{0,1:T(8,128)} fusion(bf16[2048,256]{1,0:T(8,128)(2,1)S(1)} %broadcast_select_fusion.2, bf16[1,4096,2048]{2,1,0:T(8,128)(2,1)} %param.10), kind=kOutput, calls=%fused_computation.9 | convolution fusion | flops 4294967296 | bytes 22020096 | tf_op jit(solution)/shard_map/dot_general | solution.py:26
  68.7 7.5 %gather_fusion.1 = bf16[2048,256]{1,0:T(8,128)(2,1)S(1)} fusion(bf16[2048,256]{1,0:T(8,128)(2,1)S(1)} %get-tuple-element.10, s32[2048]{0:T(1024)S(1)} %fusion.36), kind=kCustom, calls=%fused_computation.1.clone | custom fusion | bytes 2105344 | tf_op jit(solution)/shard_map/jit(_take)/gather | solution.py:53
  76.7 10.6 %fusion.9 = f32[4096,256]{0,1:T(8,128)} fusion(bf16[2048,256]{1,0:T(8,128)(2,1)S(1)} %broadcast_select_fusion.1, bf16[1,4096,2048]{2,1,0:T(8,128)(2,1)} %param.10), kind=kOutput, calls=%fused_computation.10 | convolution fusion | flops 4294967296 | bytes 22020096 | tf_op jit(solution)/shard_map/dot_general | solution.py:26
  87.4 7.5 %gather_fusion.2 = bf16[2048,256]{1,0:T(8,128)(2,1)S(1)} fusion(bf16[2048,256]{1,0:T(8,128)(2,1)S(1)} %get-tuple-element.11, s32[2048]{0:T(1024)S(1)} %fusion.37), kind=kCustom, calls=%fused_computation.2.clone | custom fusion | bytes 2105344 | tf_op jit(solution)/shard_map/jit(_take)/gather | solution.py:53
  95.3 10.6 %fusion.12 = f32[4096,256]{0,1:T(8,128)} fusion(bf16[2048,256]{1,0:T(8,128)(2,1)S(1)} %broadcast_select_fusion, bf16[1,4096,2048]{2,1,0:T(8,128)(2,1)} %param.10), kind=kOutput, calls=%fused_computation.11 | convolution fusion | flops 4294967296 | bytes 22020096 | tf_op jit(solution)/shard_map/dot_general | solution.py:26
  106.8 20.3 %all_gather.10 = bf16[1,3,256,256]{3,2,1,0:T(8,128)(2,1)S(1)} all-gather(bf16[1,3,64,256]{3,2,1,0:T(8,128)(2,1)S(1)} %copy-done.11), channel_id=1, replica_groups=mesh['row'=4,'col'=2,'pole'=4] {'row'}, dimensions={2}, use_global_device_ids=true | all-gather | bytes 491520 | tf_op jit(solution)/shard_map/all_gather | solution.py:38
  127.2 24.6 %reduce-scatter.6.cloned.1.call-done = f32[1024,256]{0,1:T(8,128)} async-done(((f32[4096,256]{0,1:T(8,128)}), f32[1024,256]{0,1:T(8,128)}) %reduce-scatter.6.cloned.1.call-update) | async-done | bytes 1048592 | tf_op jit(solution)/shard_map/reduce_scatter | solution.py:58
  151.8 79.5 %reduce-scatter.8.cloned.1.call-done = f32[1024,256]{0,1:T(8,128)} async-done(((f32[4096,256]{0,1:T(8,128)}), f32[1024,256]{0,1:T(8,128)}) %reduce-scatter.8.cloned.1.call-update) | async-done | bytes 1048592 | tf_op jit(solution)/shard_map/reduce_scatter | solution.py:58
  231.3 2.2 convolution_add_fusion.2
  233.6 2.5 convolution_bitcast_fusion.6
  236.1 1.3 convolution_bitcast_fusion.4
  237.4 73.4 %reduce-scatter.10.cloned.1.call-done = f32[1024,256]{0,1:T(8,128)} async-done(((f32[4096,256]{0,1:T(8,128)}), f32[1024,256]{0,1:T(8,128)}) %reduce-scatter.10.cloned.1.call-update) | async-done | bytes 1048592 | tf_op jit(solution)/shard_map/reduce_scatter | solution.py:58
  310.8 2.1 convolution_add_fusion.1
  316.6 0.9 pad_maximum_fusion
  317.5 1.5 convolution_bitcast_fusion.8
  320.6 2.6 maximum_multiply_fusion
  323.3 31.1 %all_gather.11 = f32[1,3,256,256]{3,2,1,0:T(8,128)S(1)} all-gather(f32[1,3,64,256]{3,2,1,0:T(8,128)S(1)} %copy-done.10), channel_id=1, replica_groups=mesh['row'=4,'col'=2,'pole'=4] {'row'}, dimensions={2}, use_global_device_ids=true | all-gather | bytes 983040 | tf_op jit(solution)/shard_map/all_gather | solution.py:41
  354.4 67.3 %all-reduce.3.cloned.1.call-done = (f32[3,256,256]{2,1,0:T(8,128)}, f32[2,256,256]{2,1,0:T(8,128)}, f32[1,256,256]{2,1,0:T(8,128)}) async-done(((f32[3,256,256]{2,1,0:T(8,128)}, f32[2,256,256]{2,1,0:T(8,128)}, f32[1,256,256]{2,1,0:T(8,128)}), (f32[3,256,256]{2,1,0:T(8,128)}, f32[2,256,256]{2,1,0:T(8,128)}, f32[1,256,256]{2,1,0:T(8,128)})) %all-reduce.3.cloned.1.call-update) | async-done | bytes 1572880 | tf_op jit(solution)/shard_map/psum | solution.py:65
  421.8 0.9 fusion.34
  422.7 1.0 slice_bitcast_fusion.2
  423.6 1.3 convolution_add_fusion.6
  424.9 1.3 convolution_add_fusion.7
  426.9 1.3 convolution_add_fusion.4
  429.2 1.3 maximum_multiply_fusion.1
  430.5 30.6 %reduce-scatter.12.cloned.1.call-done = f32[3,256,256]{1,2,0:T(8,128)} async-done(((f32[3,1024,256]{1,2,0:T(8,128)}), f32[3,256,256]{1,2,0:T(8,128)}) %reduce-scatter.12.cloned.1.call-update) | async-done | bytes 786448 | tf_op jit(solution)/shard_map/reduce_scatter | solution.py:96
  461.1 2.3 copy.18
  463.4 20.6 %reduce-scatter.14.cloned.1.call-done = f32[3,16,256]{2,1,0:T(8,128)} async-done(((f32[3,64,256]{2,1,0:T(8,128)}), f32[3,16,256]{2,1,0:T(8,128)}) %reduce-scatter.14.cloned.1.call-update) | async-done | bytes 49168 | tf_op jit(solution)/shard_map/reduce_scatter | solution.py:97
  (64 shorter events, 9.8 us)
Async XLA Ops:
  7.2 38.2 %all-gather.2.cloned.1.call-start = ((), (), s32[]{:S(2)}) async-start(), calls=%async_computation.5 | async-start | bytes 3145728 | tf_op jit(solution)/shard_map/all_gather | solution.py:46
  7.9 143.9 %reduce-scatter.6.cloned.1.call-start = ((), (), s32[]{:S(2)}) async-start(), calls=%async_computation.6 | async-start | bytes 5242880 | tf_op jit(solution)/shard_map/reduce_scatter | solution.py:58
  58.1 10.5 %copy-start.5 = (bf16[2048,256]{1,0:T(8,128)(2,1)}, bf16[2048,256]{1,0:T(8,128)(2,1)S(1)}, u32[]{:S(2)}) copy-start(bf16[2048,256]{1,0:T(8,128)(2,1)S(1)} %broadcast_select_fusion.2) | copy-start | bytes 3145732
  68.6 162.7 %reduce-scatter.8.cloned.1.call-start = ((), (), s32[]{:S(2)}) async-start(), calls=%async_computation.7 | async-start | bytes 5242880 | tf_op jit(solution)/shard_map/reduce_scatter | solution.py:58
  76.7 10.6 %copy-start.3 = (bf16[2048,256]{1,0:T(8,128)(2,1)}, bf16[2048,256]{1,0:T(8,128)(2,1)S(1)}, u32[]{:S(2)}) copy-start(bf16[2048,256]{1,0:T(8,128)(2,1)S(1)} %broadcast_select_fusion.1) | copy-start | bytes 3145732
  87.3 223.5 %reduce-scatter.10.cloned.1.call-start = ((), (), s32[]{:S(2)}) async-start(), calls=%async_computation.8 | async-start | bytes 5242880 | tf_op jit(solution)/shard_map/reduce_scatter | solution.py:58
  95.3 140.8 %copy-start.1 = (bf16[2048,256]{1,0:T(8,128)(2,1)}, bf16[2048,256]{1,0:T(8,128)(2,1)S(1)}, u32[]{:S(2)}) copy-start(bf16[2048,256]{1,0:T(8,128)(2,1)S(1)} %broadcast_select_fusion) | copy-start | bytes 3145732
  105.9 0.9 copy-start.11
  105.9 315.8 %all-reduce.3.cloned.1.call-start = ((), (), s32[]{:S(2)}) async-start(), calls=%async_computation.11 | async-start | bytes 3145728 | tf_op jit(solution)/shard_map/psum | solution.py:65
  151.8 159.0 %copy-start = (f32[1024,256]{0,1:T(8,128)S(1)}, f32[1024,256]{0,1:T(8,128)}, u32[]{:S(2)}) copy-start(f32[1024,256]{0,1:T(8,128)} %reduce-scatter.6.cloned.1.call-done) | copy-start | bytes 3145732
  310.8 2.8 copy-start.2
  310.8 3.6 copy-start.4
  312.9 2.2 copy-start.8
  312.9 3.7 copy-start.7
  313.6 3.9 copy-start.6
  315.1 4.6 copy-start.12
  319.0 142.1 %reduce-scatter.12.cloned.1.call-start = ((), (), s32[]{:S(2)}) async-start(), calls=%async_computation.9 | async-start | bytes 3932160 | tf_op jit(solution)/shard_map/reduce_scatter | solution.py:96
  320.6 2.6 copy-start.10
  323.2 160.7 %reduce-scatter.14.cloned.1.call-start = ((), (), s32[]{:S(2)}) async-start(), calls=%async_computation.10 | async-start | bytes 245760 | tf_op jit(solution)/shard_map/reduce_scatter | solution.py:97
  421.8 6.5 %copy-start.9 = (f32[2,256,256]{2,1,0:T(8,128)S(1)}, f32[2,256,256]{2,1,0:T(8,128)}, u32[]{:S(2)}) copy-start(f32[2,256,256]{2,1,0:T(8,128)} %get-tuple-element.8) | copy-start | bytes 1572868
Sparse Core Ops, SparseCore 0:
  9.5 35.8 all-gather.1
  68.8 82.9 reduce-scatter.5
  154.1 77.2 reduce-scatter.7
  233.5 77.2 reduce-scatter.9
  319.2 102.5 all-reduce.2
  424.1 36.9 reduce-scatter.11
  464.1 19.7 reduce-scatter.13
where the time goes:
time: 491 us
  waiting for transfers between devices  326 us (66%)
  blocking collectives  51.5 us (10%)
  matrix products  49.5 us (10%)
  local copies, waits for them, and re-layouts  31.8 us (6%)
  between operations  20.9 us (4%)
  other arithmetic  10.7 us (2%)
    reduce_scatter x3, waiting for transfers between devices, shards(): lax.psum_scatter(window_term(window_block, aligned), 'row', scatter_dimen...  178 us
    psum x1, waiting for transfers between devices, shards(): stacked = lax.psum(jnp.stack(partials + [congruence]), ('row', 'col'))  67.3 us
    dot_general x3, matrix products, window_term(): return jnp.dot(window_block, aligned, preferred_element_type=jnp.float32)  31.7 us
    all_gather x1, blocking collectives, shards(): lax.all_gather(diag_inverse, 'row', axis=2, tiled=True)  31.1 us
    reduce_scatter x1, waiting for transfers between devices, shards(): lax.psum_scatter(column_terms, 'pole', scatter_dimension=1, tiled=True)  30.6 us
    all_gather x1, waiting for transfers between devices, shards(): slot_panels = lax.all_gather(panels, 'col', axis=1, tiled=True)[0]  29.3 us
    gather x3, local copies, waits for them, and re-layouts, shards(): jnp.take(received, row_map[current] - row_index * band_rows, axis=0)  24 us
    reduce_scatter x1, waiting for transfers between devices, shards(): lax.psum_scatter(diagonal_terms, 'pole', scatter_dimension=1, tiled=True)  20.6 us
  transfers between devices with their start and end apart: 7, of which 7 were waited for; matrix products, arithmetic and copies ran while one was open for 12% of the time, Pallas kernels for 0%

commit v1 on v0

--- a/solution.py
+++ b/solution.py
@@ -62,7 +62,9 @@
         for earlier in range(current):
             y_window = y_window + precise(columns[earlier], factors[pair_index(current, earlier)])
         congruence = precise(own_rows.T, y_window)
-        stacked = lax.psum(jnp.stack(partials + [congruence]), ("row", "col"))
+        stacked = jnp.stack(partials + [congruence])
+        for over in ("row", "col"):
+            stacked = lax.psum(stacked, over)
         summed_cross = stacked[:current]
         summed_own = stacked[current]
         y_blocks = []

time: 491 us -> 512 us (1.043)
  waiting for transfers between devices: 326 us -> 360 us
  blocking collectives: 51.5 us -> 38.2 us
    psum x1 -> x2, waiting for transfers between devices: 67.3 us -> 100 us  [shards(): stacked = lax.psum(stacked, over)]
    all_gather x1, blocking collectives: 31.1 us -> 17.9 us  [shards(): lax.all_gather(diag_inverse, 'row', axis=2, tiled=True)]
  transfers between devices with their start and end apart: 7 -> 8, of which waited for: 7 -> 8; matrix products, arithmetic and copies ran while one was open for 12% -> 12% of each run, Pallas kernels for 0% -> 0%
where the time goes in v1:
time: 512 us
  waiting for transfers between devices  360 us (70%)
  matrix products  49.6 us (10%)
  blocking collectives  38.2 us (7%)
  local copies, waits for them, and re-layouts  31.8 us (6%)
  between operations  20.9 us (4%)
  other arithmetic  10.9 us (2%)
    reduce_scatter x3, waiting for transfers between devices, shards(): lax.psum_scatter(window_term(window_block, aligned), 'row', scatter_dimen...  178 us
    psum x2, waiting for transfers between devices, shards(): stacked = lax.psum(stacked, over)  100 us
    dot_general x3, matrix products, window_term(): return jnp.dot(window_block, aligned, preferred_element_type=jnp.float32)  31.7 us
    reduce_scatter x1, waiting for transfers between devices, shards(): lax.psum_scatter(column_terms, 'pole', scatter_dimension=1, tiled=True)  31.5 us
    all_gather x1, waiting for transfers between devices, shards(): slot_panels = lax.all_gather(panels, 'col', axis=1, tiled=True)[0]  29.3 us
    gather x3, local copies, waits for them, and re-layouts, shards(): jnp.take(received, row_map[current] - row_index * band_rows, axis=0)  24 us
    reduce_scatter x1, waiting for transfers between devices, shards(): lax.psum_scatter(diagonal_terms, 'pole', scatter_dimension=1, tiled=True)  20.5 us
    all_gather x1, blocking collectives, shards(): lax.all_gather(upper_blocks.astype(jnp.float32), 'row', axis=2, tiled=True)  20.3 us
  transfers between devices with their start and end apart: 8, of which 8 were waited for; matrix products, arithmetic and copies ran while one was open for 12% of the time, Pallas kernels for 0%

profile of v1, /device:TPU:0, one launch (start us, length us, event | category | flops | bytes accessed | tf_op | source)
XLA Modules:
  0.0 511.7 jit_solution(18328406704350297020)
XLA Ops:
  7.9 1.4 fusion.45
  16.0 29.3 %all-gather.2.cloned.1.call-done = bf16[1,2,2048,256]{3,2,0,1:T(8,128)(2,1)} async-done(((bf16[1,1,2048,256]{3,2,0,1:T(8,128)(2,1)}), bf16[1,2,2048,256]{3,2,0,1:T(8,128)(2,1)}) %all-gather.2.cloned.1.call-update) | async-done | bytes 2097168 | tf_op jit(solution)/shard_map/all_gather | solution.py:46
  45.4 2.3 dynamic-slice_bitcast_fusion.1
  47.6 9.0 %gather_fusion = bf16[2048,256]{1,0:T(8,128)(2,1)} fusion(bf16[2048,256]{1,0:T(8,128)(2,1)S(1)} %get-tuple-element.15, s32[2048]{0:T(1024)S(1)} %fusion.35), kind=kCustom, calls=%fused_computation.clone | custom fusion | bytes 2105344 | tf_op jit(solution)/shard_map/jit(_take)/gather | solution.py:53
  56.6 1.5 broadcast_select_fusion.2
  58.1 10.5 %fusion.6 = f32[4096,256]{0,1:T(8,128)} fusion(bf16[2048,256]{1,0:T(8,128)(2,1)S(1)} %broadcast_select_fusion.2, bf16[1,4096,2048]{2,1,0:T(8,128)(2,1)} %param.10), kind=kOutput, calls=%fused_computation.9 | convolution fusion | flops 4294967296 | bytes 22020096 | tf_op jit(solution)/shard_map/dot_general | solution.py:26
  68.7 7.5 %gather_fusion.1 = bf16[2048,256]{1,0:T(8,128)(2,1)S(1)} fusion(bf16[2048,256]{1,0:T(8,128)(2,1)S(1)} %get-tuple-element.13, s32[2048]{0:T(1024)S(1)} %fusion.36), kind=kCustom, calls=%fused_computation.1.clone | custom fusion | bytes 2105344 | tf_op jit(solution)/shard_map/jit(_take)/gather | solution.py:53
  76.7 10.6 %fusion.9 = f32[4096,256]{0,1:T(8,128)} fusion(bf16[2048,256]{1,0:T(8,128)(2,1)S(1)} %broadcast_select_fusion.1, bf16[1,4096,2048]{2,1,0:T(8,128)(2,1)} %param.10), kind=kOutput, calls=%fused_computation.10 | convolution fusion | flops 4294967296 | bytes 22020096 | tf_op jit(solution)/shard_map/dot_general | solution.py:26
  87.4 7.5 %gather_fusion.2 = bf16[2048,256]{1,0:T(8,128)(2,1)S(1)} fusion(bf16[2048,256]{1,0:T(8,128)(2,1)S(1)} %get-tuple-element.14, s32[2048]{0:T(1024)S(1)} %fusion.37), kind=kCustom, calls=%fused_computation.2.clone | custom fusion | bytes 2105344 | tf_op jit(solution)/shard_map/jit(_take)/gather | solution.py:53
  95.4 10.6 %fusion.12 = f32[4096,256]{0,1:T(8,128)} fusion(bf16[2048,256]{1,0:T(8,128)(2,1)S(1)} %broadcast_select_fusion, bf16[1,4096,2048]{2,1,0:T(8,128)(2,1)} %param.10), kind=kOutput, calls=%fused_computation.11 | convolution fusion | flops 4294967296 | bytes 22020096 | tf_op jit(solution)/shard_map/dot_general | solution.py:26
  106.8 20.3 %all_gather.10 = bf16[1,3,256,256]{3,2,1,0:T(8,128)(2,1)S(1)} all-gather(bf16[1,3,64,256]{3,2,1,0:T(8,128)(2,1)S(1)} %copy-done.11), channel_id=1, replica_groups=mesh['row'=4,'col'=2,'pole'=4] {'row'}, dimensions={2}, use_global_device_ids=true | all-gather | bytes 491520 | tf_op jit(solution)/shard_map/all_gather | solution.py:38
  127.2 24.6 %reduce-scatter.6.cloned.1.call-done = f32[1024,256]{0,1:T(8,128)} async-done(((f32[4096,256]{0,1:T(8,128)}), f32[1024,256]{0,1:T(8,128)}) %reduce-scatter.6.cloned.1.call-update) | async-done | bytes 1048592 | tf_op jit(solution)/shard_map/reduce_scatter | solution.py:58
  151.8 79.6 %reduce-scatter.8.cloned.1.call-done = f32[1024,256]{0,1:T(8,128)} async-done(((f32[4096,256]{0,1:T(8,128)}), f32[1024,256]{0,1:T(8,128)}) %reduce-scatter.8.cloned.1.call-update) | async-done | bytes 1048592 | tf_op jit(solution)/shard_map/reduce_scatter | solution.py:58
  231.3 2.2 convolution_add_fusion.2
  233.6 2.5 convolution_bitcast_fusion.6
  236.1 1.3 convolution_bitcast_fusion.4
  237.5 73.4 %reduce-scatter.10.cloned.1.call-done = f32[1024,256]{0,1:T(8,128)} async-done(((f32[4096,256]{0,1:T(8,128)}), f32[1024,256]{0,1:T(8,128)}) %reduce-scatter.10.cloned.1.call-update) | async-done | bytes 1048592 | tf_op jit(solution)/shard_map/reduce_scatter | solution.py:58
  310.8 2.1 convolution_add_fusion.1
  316.6 0.9 pad_maximum_fusion
  317.6 1.5 convolution_bitcast_fusion.8
  319.1 69.7 %all-reduce.5.cloned.1.call-done = (f32[3,256,256]{2,1,0:T(8,128)}, f32[2,256,256]{2,1,0:T(8,128)}, f32[1,256,256]{2,1,0:T(8,128)}) async-done(((f32[3,256,256]{2,1,0:T(8,128)}, f32[2,256,256]{2,1,0:T(8,128)}, f32[1,256,256]{2,1,0:T(8,128)}), (f32[3,256,256]{2,1,0:T(8,128)}, f32[2,256,256]{2,1,0:T(8,128)}, f32[1,256,256]{2,1,0:T(8,128)})) %all-reduce.5.cloned.1.call-update) | async-done | bytes 1572880 | tf_op jit(solution)/shard_map/psum | solution.py:67
  390.4 2.6 maximum_multiply_fusion
  393.2 17.9 %all_gather.11 = f32[1,3,256,256]{3,2,1,0:T(8,128)S(1)} all-gather(f32[1,3,64,256]{3,2,1,0:T(8,128)S(1)} %copy-done.10), channel_id=1, replica_groups=mesh['row'=4,'col'=2,'pole'=4] {'row'}, dimensions={2}, use_global_device_ids=true | all-gather | bytes 983040 | tf_op jit(solution)/shard_map/all_gather | solution.py:41
  411.1 30.6 %all-reduce.7.cloned.1.call-done = (f32[3,256,256]{2,1,0:T(8,128)}, f32[2,256,256]{2,1,0:T(8,128)}, f32[1,256,256]{2,1,0:T(8,128)}) async-done(((f32[3,256,256]{2,1,0:T(8,128)}, f32[2,256,256]{2,1,0:T(8,128)}, f32[1,256,256]{2,1,0:T(8,128)}), (f32[3,256,256]{2,1,0:T(8,128)}, f32[2,256,256]{2,1,0:T(8,128)}, f32[1,256,256]{2,1,0:T(8,128)})) %all-reduce.7.cloned.1.call-update) | async-done | bytes 1572880 | tf_op jit(solution)/shard_map/psum | solution.py:67
  442.6 1.0 slice_bitcast_fusion.2
  443.6 1.3 convolution_add_fusion.6
  444.9 1.3 convolution_add_fusion.7
  446.8 1.3 convolution_add_fusion.4
  449.2 1.3 maximum_multiply_fusion.1
  450.5 31.5 %reduce-scatter.12.cloned.1.call-done = f32[3,256,256]{1,2,0:T(8,128)} async-done(((f32[3,1024,256]{1,2,0:T(8,128)}), f32[3,256,256]{1,2,0:T(8,128)}) %reduce-scatter.12.cloned.1.call-update) | async-done | bytes 786448 | tf_op jit(solution)/shard_map/reduce_scatter | solution.py:98
  482.0 2.3 copy.18
  484.3 20.5 %reduce-scatter.14.cloned.1.call-done = f32[3,16,256]{2,1,0:T(8,128)} async-done(((f32[3,64,256]{2,1,0:T(8,128)}), f32[3,16,256]{2,1,0:T(8,128)}) %reduce-scatter.14.cloned.1.call-update) | async-done | bytes 49168 | tf_op jit(solution)/shard_map/reduce_scatter | solution.py:99
  (67 shorter events, 10.8 us)
Async XLA Ops:
  7.2 38.2 %all-gather.2.cloned.1.call-start = ((), (), s32[]{:S(2)}) async-start(), calls=%async_computation.5 | async-start | bytes 3145728 | tf_op jit(solution)/shard_map/all_gather | solution.py:46
  7.9 143.9 %reduce-scatter.6.cloned.1.call-start = ((), (), s32[]{:S(2)}) async-start(), calls=%async_computation.6 | async-start | bytes 5242880 | tf_op jit(solution)/shard_map/reduce_scatter | solution.py:58
  58.1 10.5 %copy-start.5 = (bf16[2048,256]{1,0:T(8,128)(2,1)}, bf16[2048,256]{1,0:T(8,128)(2,1)S(1)}, u32[]{:S(2)}) copy-start(bf16[2048,256]{1,0:T(8,128)(2,1)S(1)} %broadcast_select_fusion.2) | copy-start | bytes 3145732
  68.7 162.7 %reduce-scatter.8.cloned.1.call-start = ((), (), s32[]{:S(2)}) async-start(), calls=%async_computation.7 | async-start | bytes 5242880 | tf_op jit(solution)/shard_map/reduce_scatter | solution.py:58
  76.7 10.6 %copy-start.3 = (bf16[2048,256]{1,0:T(8,128)(2,1)}, bf16[2048,256]{1,0:T(8,128)(2,1)S(1)}, u32[]{:S(2)}) copy-start(bf16[2048,256]{1,0:T(8,128)(2,1)S(1)} %broadcast_select_fusion.1) | copy-start | bytes 3145732
  87.3 223.5 %reduce-scatter.10.cloned.1.call-start = ((), (), s32[]{:S(2)}) async-start(), calls=%async_computation.8 | async-start | bytes 5242880 | tf_op jit(solution)/shard_map/reduce_scatter | solution.py:58
  95.4 140.8 %copy-start.1 = (bf16[2048,256]{1,0:T(8,128)(2,1)}, bf16[2048,256]{1,0:T(8,128)(2,1)S(1)}, u32[]{:S(2)}) copy-start(bf16[2048,256]{1,0:T(8,128)(2,1)S(1)} %broadcast_select_fusion) | copy-start | bytes 3145732
  106.0 0.9 copy-start.11
  106.0 282.8 %all-reduce.5.cloned.1.call-start = ((), (), s32[]{:S(2)}) async-start(), calls=%async_computation.11 | async-start | bytes 3145728 | tf_op jit(solution)/shard_map/psum | solution.py:67
  151.8 159.1 %copy-start = (f32[1024,256]{0,1:T(8,128)S(1)}, f32[1024,256]{0,1:T(8,128)}, u32[]{:S(2)}) copy-start(f32[1024,256]{0,1:T(8,128)} %reduce-scatter.6.cloned.1.call-done) | copy-start | bytes 3145732
  310.8 2.8 copy-start.2
  310.8 3.6 copy-start.4
  312.9 2.2 copy-start.8
  312.9 3.7 copy-start.7
  313.7 3.9 copy-start.6
  316.0 73.5 %copy-start.12 = (f32[4]{0:T(128)S(1)}, f32[4]{0:T(128)}, u32[]{:S(2)}) copy-start(f32[4]{0:T(128)} %param.16) | copy-start | bytes 52
  319.1 122.7 %all-reduce.7.cloned.1.call-start = ((), (), s32[]{:S(2)}) async-start(), calls=%async_computation.12 | async-start | bytes 3145728 | tf_op jit(solution)/shard_map/psum | solution.py:67
  388.8 93.2 %reduce-scatter.12.cloned.1.call-start = ((), (), s32[]{:S(2)}) async-start(), calls=%async_computation.9 | async-start | bytes 3932160 | tf_op jit(solution)/shard_map/reduce_scatter | solution.py:98
  390.4 2.7 copy-start.10
  393.1 111.8 %reduce-scatter.14.cloned.1.call-start = ((), (), s32[]{:S(2)}) async-start(), calls=%async_computation.10 | async-start | bytes 245760 | tf_op jit(solution)/shard_map/reduce_scatter | solution.py:99
  441.7 6.5 %copy-start.9 = (f32[2,256,256]{2,1,0:T(8,128)S(1)}, f32[2,256,256]{2,1,0:T(8,128)}, u32[]{:S(2)}) copy-start(f32[2,256,256]{2,1,0:T(8,128)} %get-tuple-element.11) | copy-start | bytes 1572868
Sparse Core Ops, SparseCore 0:
  9.5 35.8 all-gather.1
  68.8 82.9 reduce-scatter.5
  154.1 77.2 reduce-scatter.7
  233.5 77.2 reduce-scatter.9
  319.2 69.5 all-reduce.4
  391.0 50.6 all-reduce.6
  444.3 37.7 reduce-scatter.11
  485.1 19.7 reduce-scatter.13
